TPU v7x, 1024 devices: a whole 8x8x8 slice. The times are simulated.
1024 devices in a mesh: replica: 32 (over x_hi, z), expert: 32 (over x_lo, y, core).
Axes of the slice: x: 8 (x_hi: 4, x_lo: 2; x = x_hi * 2 + x_lo), y: 8, z: 8, core: 2. Of those that a mesh axis runs over, the one named last changes fastest.
Arguments:
- master: float32 [32, 32, 32, 2, 768], P('replica', 'expert'), may hold values from -6 to 6
- first_moment: float32 [32, 32, 32, 2, 768], P('replica', 'expert'), may hold values from -4 to 4
- second_moment: float32 [32, 32, 32, 2, 768], P('replica', 'expert'), may hold values from 0.001 to 1
- gradient: bfloat16 [32, 32, 32, 2, 768], P('replica', 'expert'), may hold values from -6 to 6
- scale_exponent: int32 [32, 32, 32, 2, 6], P('replica', 'expert'), may hold values from 3 to 7
- slot_expert: int32 [32, 32, 32], P('replica', 'expert'), may hold values from 0 to 31, each once within a row
- expert_owner: int32 [32], replicated, may hold values from 0 to 31, each once
- serving_weights: bfloat16 [32, 2048, 768], P('expert'), may hold values from -6 to 6
Outputs:
- master_out: float32 [32, 32, 32, 2, 768], P('replica', 'expert')
- first_out: float32 [32, 32, 32, 2, 768], P('replica', 'expert')
- second_out: float32 [32, 32, 32, 2, 768], P('replica', 'expert')
- serving_out: bfloat16 [32, 2048, 768], P('expert')
Inputs may be any that keep to these rules, and one draw needn't show every extreme that they name: `slot_expert`: each row along the last dimension names every expert once. `expert_owner`: names every owner once.
All inputs are finite; a program needn't handle non-finite values.
Results may differ from a plain program's by a relative error of at most 0.0015.
Values may be sent and summed in bfloat16 or wider, within the bound.
No kernel may reach another device: no remote copies, remote signals or barrier semaphores. Data moves between devices by JAX's collectives and lax.ppermute only.
A program may use at most 64 MiB of HBM per device.

v0:
```python
import jax
import jax.numpy as jnp
from jax import lax
from jax.sharding import PartitionSpec as P


def apply_rows(serving_rows, coded_rows, scale_rows):
    count = coded_rows.shape[0]
    blocks = scale_rows.shape[1]
    shaped = coded_rows.reshape(count, blocks, -1).astype(jnp.float32)
    added = (shaped * scale_rows.astype(jnp.float32)[..., None]).reshape(count, -1)
    return (serving_rows.astype(jnp.float32) + added).astype(jnp.bfloat16)


def shards(
    master,
    first_moment,
    second_moment,
    gradient,
    scale_exponent,
    slot_expert,
    expert_owner,
    serving_weights,
):
    grad_full = gradient.astype(jnp.float32)
    first_out = 0.9 * first_moment + 0.1 * grad_full
    second_out = 0.95 * second_moment + 0.05 * grad_full * grad_full
    corr_first = 1.0 - 0.9**10
    corr_second = 1.0 - 0.95**10
    update = first_out / corr_first / (jnp.sqrt(second_out / corr_second) + 1e-08) + 0.1 * master
    delta = -0.1 * update
    master_out = master + delta
    slots = master.shape[2]
    sub_rows = master.shape[3]
    columns = master.shape[4]
    blocks = scale_exponent.shape[4]
    scale = jnp.exp2(-scale_exponent[0, 0].astype(jnp.float32))
    shaped = delta[0, 0].reshape(slots, sub_rows, blocks, columns // blocks)
    coded = (
        jnp.clip(shaped / scale[..., None], -8.0, 8.0)
        .astype(jnp.bfloat16)
        .reshape(slots, sub_rows, columns)
    )
    scale_wire = scale.astype(jnp.bfloat16)
    target = expert_owner[slot_expert[0, 0]]
    ordering = jnp.zeros((slots,), jnp.int32).at[target].set(jnp.arange(slots, dtype=jnp.int32))
    coded_sent = coded[ordering]
    scale_sent = scale_wire[ordering]
    coded_recv = lax.all_to_all(coded_sent, "expert", split_axis=0, concat_axis=0, tiled=True)
    scale_recv = lax.all_to_all(scale_sent, "expert", split_axis=0, concat_axis=0, tiled=True)
    piece_rows = slots * sub_rows
    coded_piece = coded_recv.reshape(piece_rows, columns)
    scale_piece = scale_recv.reshape(piece_rows, blocks)
    serving_flat = serving_weights[0]
    new_rows = apply_rows(
        serving_flat,
        lax.all_gather(coded_piece, "replica", axis=0, tiled=True),
        lax.all_gather(scale_piece, "replica", axis=0, tiled=True),
    )
    return (master_out, first_out, second_out, new_rows[None])


def solution(mesh):
    in_specs = (
        P("replica", "expert", None, None, None),
        P("replica", "expert", None, None, None),
        P("replica", "expert", None, None, None),
        P("replica", "expert", None, None, None),
        P("replica", "expert", None, None, None),
        P("replica", "expert", None),
        P(),
        P("expert", None, None),
    )
    out_specs = (
        P("replica", "expert", None, None, None),
        P("replica", "expert", None, None, None),
        P("replica", "expert", None, None, None),
        P("expert", None, None),
    )
    return jax.shard_map(shards, mesh=mesh, in_specs=in_specs, out_specs=out_specs, check_vma=False)
```

profile of v0, /device:TPU:2, one launch (start us, length us, event | category | flops | bytes accessed | tf_op | source)
XLA Modules:
  0.0 164.8 jit_solution(8352918829352747117)
XLA Ops:
  7.2 0.0 copy-start
  7.2 0.0 all-gather.3.cloned.1.call-start
  7.2 0.7 fusion.8
  7.9 0.1 copy.42
  8.0 0.1 div.31
  8.2 0.7 fusion.4
  8.9 0.0 copy-done
  8.9 0.7 gather_fusion
  9.6 0.7 scatter_custom_fusion
  10.3 2.7 %clamp_convert_fusion = (bf16[32,2,768]{2,1,0:T(2,128)(2,1)S(1)}, f32[1,1,32,2,768]{4,3,2,1,0:T(2,128)S(1)}, f32[1,1,32,2,768]{4,3,2,1,0:T(2,128)}, f32[1,1,32,2,768]{4,3,2,1,0:T(2,128)}) fusion(f32[32,2,768]{2,0,1:T(8,128)S(1)} %div.32, f32[1,1,32,2,768]{4,3,2,1,0:T(2,128)} %param.8, bf16[1,1,32,2,768]{4,3,2,1,0:T(2,128)(2,1)} %param.11, ...), kind=kLoop, calls=%fused_computation.12 | loop fusion | flops 884736 | bytes 1572864 | tf_op jit(solution)/shard_map/convert_element_type | solution.py:41
  13.0 0.8 gather_fusion.1
  13.7 23.8 %all_to_all.10 = bf16[32,2,768]{2,1,0:T(2,128)(2,1)S(1)} all-to-all(bf16[32,2,768]{2,1,0:T(2,128)(2,1)S(1)} %gather_fusion.1), channel_id=1, replica_groups=mesh['replica'=32,'expert'=32] {'expert'}, dimensions={0} | all-to-all | bytes 196608 | tf_op jit(solution)/shard_map/all_to_all | solution.py:49
  37.5 0.7 reshape.77
  38.2 0.0 all-gather.3.cloned.1.call-update
  38.2 0.1 copy.44
  38.3 1.2 gather_fusion.2
  39.5 4.6 %all-to-all-start.1 = ((bf16[32,2,6]{2,1,0:T(2,128)(2,1)}), bf16[32,2,6]{2,1,0:T(2,128)(2,1)S(1)}, u32[]{:S(2)}, u32[]{:S(2)}) async-start(bf16[32,2,6]{2,1,0:T(2,128)(2,1)} %gather_fusion.2), calls=%async_computation.1 | async-start | bytes 32768 | tf_op jit(solution)/shard_map/all_to_all | solution.py:50
  44.2 1.8 %add.50 = f32[1,1,32,2,768]{4,3,2,1,0:T(2,128)} add(f32[1,1,32,2,768]{4,3,2,1,0:T(2,128)} %param.8, f32[1,1,32,2,768]{4,3,2,1,0:T(2,128)S(1)} %get-tuple-element.9) | non-fusion elementwise | flops 49152 | bytes 589824 | tf_op jit(solution)/shard_map/add | solution.py:32
  46.0 5.2 %all-to-all-done.1 = bf16[32,2,6]{2,1,0:T(2,128)(2,1)S(1)} async-done(((bf16[32,2,6]{2,1,0:T(2,128)(2,1)}), bf16[32,2,6]{2,1,0:T(2,128)(2,1)S(1)}, u32[]{:S(2)}, u32[]{:S(2)}) %all-to-all-start.1) | async-done | bytes 800 | tf_op jit(solution)/shard_map/all_to_all | solution.py:50
  51.2 0.1 copy.45
  51.3 89.9 %all-gather = bf16[32,64,6]{1,2,0:T(8,128)(2,1)S(1)} all-gather(bf16[1,64,6]{1,2,0:T(8,128)(2,1)S(1)} %copy.45), channel_id=1, replica_groups=mesh['replica'=32,'expert'=32] {'replica'}, dimensions={0}, use_global_device_ids=true | all-gather | bytes 25344 | tf_op jit(solution)/shard_map/all_gather | solution.py:58
  141.2 0.1 reshape.116
  141.3 3.4 %mul.55 = f32[2048,6,128]{0,2,1:T(8,128)} broadcast(f32[2048,6]{0,1:T(8,128)S(1)} %reshape.116), dimensions={0,1} | broadcast | bytes 6340608 | tf_op jit(solution)/shard_map/mul | solution.py:11
  144.7 0.0 copy-start.1
  144.7 6.7 %copy.47 = f32[2048,768]{1,0:T(8,128)} copy(f32[2048,768]{0,1:T(8,128)} %bitcast.27) | data formatting | bytes 12582912 | tf_op jit(solution)/shard_map/mul | solution.py:11
  151.4 0.0 all-gather.3.cloned.1.call-done
  151.4 0.0 copy-done.1
  151.4 6.5 %fusion.1 = bf16[1,2048,768]{2,1,0:T(8,128)(2,1)} fusion(f32[2048,768]{1,0:T(8,128)} %copy.47, bf16[2048,768]{1,0:T(8,128)(2,1)} %all-gather.3.cloned.1.call-done, bf16[1,2048,768]{2,1,0:T(8,128)(2,1)S(1)} %copy-done.1), kind=kLoop, calls=%fused_computation.6 | loop fusion | flops 7864320 | bytes 15728640 | tf_op jit(solution)/shard_map/broadcast_in_dim | solution.py:60
  (7 shorter events, 0.1 us)
Async XLA Ops:
  7.2 1.7 %copy-start = (s32[32]{0:T(128)S(1)}, s32[32]{0:T(128)}, u32[]{:S(2)}) copy-start(s32[32]{0:T(128)} %param.14) | copy-start | bytes 388
  7.2 144.3 %all-gather.3.cloned.1.call-start = ((), (), s32[]{:S(2)}) async-start(), calls=%async_computation.2 | async-start | bytes 3244032 | tf_op jit(solution)/shard_map/all_gather | solution.py:57
  39.5 11.7 %all-to-all-start.1 = ((bf16[32,2,6]{2,1,0:T(2,128)(2,1)}), bf16[32,2,6]{2,1,0:T(2,128)(2,1)S(1)}, u32[]{:S(2)}, u32[]{:S(2)}) async-start(bf16[32,2,6]{2,1,0:T(2,128)(2,1)} %gather_fusion.2), calls=%async_computation.1 | async-start | bytes 32768 | tf_op jit(solution)/shard_map/all_to_all | solution.py:50
  144.7 6.7 %copy-start.1 = (bf16[1,2048,768]{2,1,0:T(8,128)(2,1)S(1)}, bf16[1,2048,768]{2,1,0:T(8,128)(2,1)}, u32[]{:S(2)}) copy-start(bf16[1,2048,768]{2,1,0:T(8,128)(2,1)} %param.15) | copy-start | bytes 9437188
Sparse Core Ops, SparseCore 0:
  38.3 98.1 all-gather.2
where the time goes:
time: 165 us
  blocking collectives  114 us (69%)
  local copies, waits for them, and re-layouts  14.7 us (9%)
  between operations  14.1 us (9%)
  other arithmetic  12.4 us (8%)
  waiting for transfers between devices  5.23 us (3%)
  starting transfers between devices  4.67 us (3%)
    all_gather x1, blocking collectives, shards(): lax.all_gather(scale_piece, 'replica', axis=0, tiled=True)  89.9 us
    all_to_all x1, blocking collectives, shards(): lax.all_to_all(coded_sent, 'expert', split_axis=0, concat_axis=0, tiled=T...  23.8 us
    mul x2, local copies, waits for them, and re-layouts, apply_rows(): shaped * scale_rows.astype(jnp.float32)[..., None]  10.1 us
    broadcast_in_dim x1, other arithmetic, shards(): return (master_out, first_out, second_out, new_rows[None])  6.49 us
    all_to_all x1, waiting for transfers between devices, shards(): lax.all_to_all(scale_sent, 'expert', split_axis=0, concat_axis=0, tiled=T...  5.21 us
    all_to_all x1, starting transfers between devices, shards(): lax.all_to_all(scale_sent, 'expert', split_axis=0, concat_axis=0, tiled=T...  4.63 us
  transfers between devices with their start and end apart: 2, of which 1 were waited for; matrix products, arithmetic and copies ran while one was open for 8% of the time, Pallas kernels for 0%

commit v1 on v0

v1 whole, which is shorter than its diff:
```python
import jax
import jax.numpy as jnp
from jax import lax
from jax.sharding import PartitionSpec as P


def shards(
    master,
    first_moment,
    second_moment,
    gradient,
    scale_exponent,
    slot_expert,
    expert_owner,
    serving_weights,
):
    grad_full = gradient.astype(jnp.float32)
    first_out = 0.9 * first_moment + 0.1 * grad_full
    second_out = 0.95 * second_moment + 0.05 * grad_full * grad_full
    corr_first = 1.0 - 0.9**10
    corr_second = 1.0 - 0.95**10
    update = first_out / corr_first / (jnp.sqrt(second_out / corr_second) + 1e-08) + 0.1 * master
    delta = -0.1 * update
    master_out = master + delta
    slots = master.shape[2]
    sub_rows = master.shape[3]
    columns = master.shape[4]
    blocks = scale_exponent.shape[4]
    limit = 8.0 * jnp.exp2(-scale_exponent[0, 0].astype(jnp.float32))
    shaped = delta[0, 0].reshape(slots, sub_rows, blocks, columns // blocks)
    added = (
        jnp.clip(shaped, -limit[..., None], limit[..., None])
        .astype(jnp.bfloat16)
        .reshape(slots, sub_rows, columns)
    )
    target = expert_owner[slot_expert[0, 0]]
    ordering = jnp.zeros((slots,), jnp.int32).at[target].set(jnp.arange(slots, dtype=jnp.int32))
    added_recv = lax.all_to_all(added[ordering], "expert", split_axis=0, concat_axis=0, tiled=True)
    piece = added_recv.reshape(slots * sub_rows, columns)
    gathered = lax.all_gather(piece, "replica", axis=0, tiled=True)
    new_rows = (serving_weights[0].astype(jnp.float32) + gathered.astype(jnp.float32)).astype(jnp.bfloat16)
    return (master_out, first_out, second_out, new_rows[None])


def solution(mesh):
    in_specs = (
        P("replica", "expert", None, None, None),
        P("replica", "expert", None, None, None),
        P("replica", "expert", None, None, None),
        P("replica", "expert", None, None, None),
        P("replica", "expert", None, None, None),
        P("replica", "expert", None),
        P(),
        P("expert", None, None),
    )
    out_specs = (
        P("replica", "expert", None, None, None),
        P("replica", "expert", None, None, None),
        P("replica", "expert", None, None, None),
        P("expert", None, None),
    )
    return jax.shard_map(shards, mesh=mesh, in_specs=in_specs, out_specs=out_specs, check_vma=False)
```

time: 165 us -> 154 us (0.933)
  the two profiles are of different devices: /device:TPU:2 before, /device:TPU:16 now
where the time goes in v1:
time: 154 us
  waiting for transfers between devices  94.9 us (62%)
  blocking collectives  24.9 us (16%)
  between operations  14.1 us (9%)
  local copies, waits for them, and re-layouts  10.5 us (7%)
  other arithmetic  9.16 us (6%)
    all_gather x1, waiting for transfers between devices, shards(): gathered = lax.all_gather(piece, 'replica', axis=0, tiled=True)  94.9 us
    all_to_all x1, blocking collectives, shards(): lax.all_to_all(added[ordering], 'expert', split_axis=0, concat_axis=0, ti...  24.9 us
    broadcast_in_dim x1, other arithmetic, shards(): return (master_out, first_out, second_out, new_rows[None])  4.38 us
  transfers between devices with their start and end apart: 1, of which 1 were waited for; matrix products, arithmetic and copies ran while one was open for 2% of the time, Pallas kernels for 0%

profile of v1, /device:TPU:16, one launch (start us, length us, event | category | flops | bytes accessed | tf_op | source)
XLA Modules:
  0.0 153.5 jit_solution(939743088381565637)
XLA Ops:
  7.2 0.0 copy-start
  7.2 0.0 copy-start.1
  7.2 0.0 all-gather.2.cloned.1.call-start
  7.2 0.9 fusion.10
  8.1 0.8 multiply_bitcast_fusion
  8.9 0.7 fusion.6
  9.5 0.0 copy-done
  9.5 0.7 gather_fusion
  10.2 0.7 scatter_custom_fusion
  10.9 0.1 copy.33
  11.1 0.1 copy.34
  11.2 0.1 max.15
  11.3 0.8 max.16
  12.1 0.1 min.15
  12.2 0.8 min.16
  13.0 1.4 fusion.5
  14.4 0.7 copy.35
  15.2 2.3 %gather_fusion.1 = bf16[32,2,768]{2,1,0:T(2,128)(2,1)} fusion(bf16[32,2,768]{2,1,0:T(2,128)(2,1)} %copy.35, s32[1024]{0:T(1024)S(1)} %pad_clamp_fusion), kind=kCustom, calls=%fused_computation.1 | custom fusion | bytes 196736 | tf_op jit(solution)/shard_map/gather | solution.py:38
  17.5 24.9 %all_to_all.5 = bf16[32,2,768]{2,1,0:T(2,128)(2,1)} all-to-all(bf16[32,2,768]{2,1,0:T(2,128)(2,1)} %gather_fusion.1), channel_id=1, replica_groups=mesh['replica'=32,'expert'=32] {'expert'}, dimensions={0} | all-to-all | bytes 196608 | tf_op jit(solution)/shard_map/all_to_all | solution.py:38
  42.3 1.6 %reshape.77 = bf16[64,768]{1,0:T(8,128)(2,1)} reshape(bf16[32,2,768]{2,1,0:T(2,128)(2,1)} %all_to_all.5) | data formatting | bytes 196608 | tf_op jit(solution)/shard_map/reshape | solution.py:39
  43.9 0.0 all-gather.2.cloned.1.call-update
  43.9 0.8 copy.37
  44.8 0.8 copy.38
  45.6 1.0 copy_add_fusion
  46.6 0.8 copy.36
  47.5 94.9 %all-gather.2.cloned.1.call-done = bf16[2048,768]{1,0:T(8,128)(2,1)} async-done(((bf16[64,768]{1,0:T(8,128)(2,1)}), bf16[2048,768]{1,0:T(8,128)(2,1)}) %all-gather.2.cloned.1.call-update) | async-done | bytes 3145744 | tf_op jit(solution)/shard_map/all_gather | solution.py:40
  142.3 0.0 copy-done.1
  142.3 4.4 %fusion.1 = bf16[1,2048,768]{2,1,0:T(8,128)(2,1)} fusion(bf16[2048,768]{1,0:T(8,128)(2,1)} %all-gather.2.cloned.1.call-done, bf16[1,2048,768]{2,1,0:T(8,128)(2,1)S(1)} %copy-done.1), kind=kLoop, calls=%fused_computation.5 | loop fusion | flops 6291456 | bytes 9437184 | tf_op jit(solution)/shard_map/broadcast_in_dim | solution.py:42
  (5 shorter events, 0.0 us)
Async XLA Ops:
  7.2 2.4 %copy-start = (s32[32]{0:T(128)S(1)}, s32[32]{0:T(128)}, u32[]{:S(2)}) copy-start(s32[32]{0:T(128)} %param.14) | copy-start | bytes 388
  7.2 135.1 %copy-start.1 = (bf16[1,2048,768]{2,1,0:T(8,128)(2,1)S(1)}, bf16[1,2048,768]{2,1,0:T(8,128)(2,1)}, u32[]{:S(2)}) copy-start(bf16[1,2048,768]{2,1,0:T(8,128)(2,1)} %param.15) | copy-start | bytes 9437188
  7.2 135.1 %all-gather.2.cloned.1.call-start = ((), (), s32[]{:S(2)}) async-start(), calls=%async_computation.1 | async-start | bytes 3244032 | tf_op jit(solution)/shard_map/all_gather | solution.py:40
Sparse Core Ops, SparseCore 0:
  44.0 98.2 all-gather.1

commit v2 on v1

--- a/solution.py
+++ b/solution.py
@@ -2,6 +2,9 @@
 import jax.numpy as jnp
 from jax import lax
 from jax.sharding import PartitionSpec as P
+
+RING = 8
+LIFT = 2.0**15
 
 
 def shards(
@@ -37,8 +40,15 @@
     ordering = jnp.zeros((slots,), jnp.int32).at[target].set(jnp.arange(slots, dtype=jnp.int32))
     added_recv = lax.all_to_all(added[ordering], "expert", split_axis=0, concat_axis=0, tiled=True)
     piece = added_recv.reshape(slots * sub_rows, columns)
-    gathered = lax.all_gather(piece, "replica", axis=0, tiled=True)
-    new_rows = (serving_weights[0].astype(jnp.float32) + gathered.astype(jnp.float32)).astype(jnp.bfloat16)
+    replicas = lax.axis_size("replica")
+    along_x = [[x * RING + z for x in range(replicas // RING)] for z in range(RING)]
+    along_z = [[x * RING + z for z in range(RING)] for x in range(replicas // RING)]
+    part = lax.all_gather(piece, "replica", axis=0, tiled=False, axis_index_groups=along_x)
+    wire = (part.astype(jnp.float32) * LIFT).astype(jnp.float16)
+    whole = lax.all_gather(wire, "replica", axis=0, tiled=False, axis_index_groups=along_z)
+    gathered = whole.astype(jnp.float32) * (1.0 / LIFT)
+    gathered = jnp.transpose(gathered, (1, 0, 2, 3)).reshape(serving_weights.shape[1:])
+    new_rows = (serving_weights[0].astype(jnp.float32) + gathered).astype(jnp.bfloat16)
     return (master_out, first_out, second_out, new_rows[None])
 
 

time: 154 us -> 94.5 us (0.61)
  the two profiles are of different devices: /device:TPU:16 before, /device:TPU:2 now
where the time goes in v2:
time: 94.5 us; the launch traced here: 94.2 us
  blocking collectives  56.5 us (60%)
  starting transfers between devices  16.8 us (18%)
  local copies, waits for them, and re-layouts  8.03 us (8%)
  other arithmetic  7.68 us (8%)
  waiting for transfers between devices  4.38 us (5%)
    all_gather x1, blocking collectives, shards(): lax.all_gather(wire, 'replica', axis=0, tiled=False, axis_index_groups=al...  40.4 us
    all_to_all x1, starting transfers between devices, shards(): lax.all_to_all(added[ordering], 'expert', split_axis=0, concat_axis=0, ti...  16.8 us
    all_gather x1, blocking collectives, shards(): lax.all_gather(piece, 'replica', axis=0, tiled=False, axis_index_groups=a...  16.2 us
    all_to_all x1, waiting for transfers between devices, shards(): lax.all_to_all(added[ordering], 'expert', split_axis=0, concat_axis=0, ti...  4.38 us
    unnamed x7, local copies, waits for them, and re-layouts  3.68 us
    convert_element_type x1, other arithmetic, shards(): (serving_weights[0].astype(jnp.float32) + gathered).astype(jnp.bfloat16)  2.36 us
  transfers between devices with their start and end apart: 1, of which 1 were waited for; matrix products, arithmetic and copies ran while one was open for 4% of the time, Pallas kernels for 0%

profile of v2, /device:TPU:2, one launch (start us, length us, event | category | flops | bytes accessed | tf_op | source)
XLA Modules:
  0.0 94.2 jit_solution(18121463159980752644)
XLA Ops:
  0.6 0.0 copy-start
  0.6 0.7 fusion.8
  1.4 0.7 multiply_bitcast_fusion
  2.1 0.7 fusion.4
  2.7 0.0 copy-done
  2.7 0.7 gather_fusion
  3.5 0.7 scatter_custom_fusion
  4.2 0.1 copy.39
  4.3 0.1 copy.40
  4.4 0.1 max.15
  4.5 0.1 max.16
  4.7 0.1 min.15
  4.8 0.1 min.16
  4.9 1.4 %fusion.3 = (bf16[32,2,768]{2,0,1:T(8,128)(2,1)S(1)}, f32[1,1,32,2,768]{4,2,3,1,0:T(8,128)S(1)}, f32[1,1,32,2,768]{4,2,3,1,0:T(8,128)S(1)}) fusion(bf16[32,2,768]{2,0,1:T(8,128)(2,1)S(1)} %min.16, bf16[32,2,768]{2,0,1:T(8,128)(2,1)S(1)} %max.16, f32[1,1,32,2,768]{4,3,2,1,0:T(2,128)} %param.8, bf16[1,1,32,2,768]{4,3,2,1,0:T(2,128)(2,1)} %param.11, ...), kind=kLoop, calls=%fused_computation.12 | loop fusion | flops 983040 | bytes 1376256 | tf_op jit(solution)/shard_map/convert_element_type | solution.py:36
  6.3 0.1 copy.41
  6.4 1.4 %gather_fusion.1 = bf16[32,2,768]{2,1,0:T(2,128)(2,1)} fusion(bf16[32,2,768]{2,1,0:T(2,128)(2,1)S(1)} %copy.41, s32[1024]{0:T(1024)S(1)} %pad_clamp_fusion), kind=kCustom, calls=%fused_computation.1 | custom fusion | bytes 196736 | tf_op jit(solution)/shard_map/gather | solution.py:41
  7.8 16.8 %all-to-all-start = ((bf16[32,2,768]{2,1,0:T(2,128)(2,1)}), bf16[32,2,768]{2,1,0:T(2,128)(2,1)S(1)}, u32[]{:S(2)}, u32[]{:S(2)}) async-start(bf16[32,2,768]{2,1,0:T(2,128)(2,1)} %gather_fusion.1), calls=%async_computation | async-start | bytes 196608 | tf_op jit(solution)/shard_map/all_to_all | solution.py:41
  24.6 0.8 copy.44
  25.4 0.8 copy.45
  26.2 1.0 %copy_add_fusion = f32[1,1,32,2,768]{4,2,3,1,0:T(8,128)S(1)} fusion(f32[1,1,32,2,768]{4,3,2,1,0:T(2,128)} %param.8, f32[1,1,32,2,768]{4,2,3,1,0:T(8,128)S(1)} %get-tuple-element.14, f32[1,1,32,2,768]{4,2,3,1,0:T(8,128)S(1)} %get-tuple-element.13), kind=kLoop, calls=%fused_computation.16 | loop fusion | flops 393216 | bytes 786432 | tf_op jit(solution)/shard_map/add | solution.py:27
  27.3 0.8 copy.43
  28.1 4.4 %all-to-all-done = bf16[32,2,768]{2,1,0:T(2,128)(2,1)S(1)} async-done(((bf16[32,2,768]{2,1,0:T(2,128)(2,1)}), bf16[32,2,768]{2,1,0:T(2,128)(2,1)S(1)}, u32[]{:S(2)}, u32[]{:S(2)}) %all-to-all-start) | async-done | bytes 98336 | tf_op jit(solution)/shard_map/all_to_all | solution.py:41
  32.5 16.2 %all_gather.9 = bf16[4,64,768]{2,1,0:T(8,128)(2,1)S(1)} all-gather(bf16[1,64,768]{2,1,0:T(8,128)(2,1)S(1)} %all_gather_reshape.3), channel_id=1, replica_groups={{0,256,512,768},{32,288,544,800},{64,320,576,832},{96,352,608,864},{128..., dimensions={0}, use_global_device_ids=true | all-gather | bytes 491520 | tf_op jit(solution)/shard_map/all_gather | solution.py:46
  48.7 0.1 multiply_convert_fusion
  48.8 40.4 %all-gather.2 = f16[32,64,768]{2,1,0:T(8,128)(2,1)S(1)} all-gather(f16[4,64,768]{2,1,0:T(8,128)(2,1)S(1)} %multiply_convert_fusion), channel_id=2, replica_groups={{0,32,64,96,128,160,192,224},{256,288,320,352,384,416,448,480},{512,544..., dimensions={0}, use_global_device_ids=true | all-gather | bytes 3538944 | tf_op jit(solution)/shard_map/all_gather | solution.py:48
  89.2 0.7 convert_multiply_fusion
  89.9 0.0 copy-start.1
  89.9 0.7 copy.42
  90.6 1.2 %copy-done.1 = bf16[1,2048,768]{2,1,0:T(8,128)(2,1)S(1)} copy-done((bf16[1,2048,768]{2,1,0:T(8,128)(2,1)S(1)}, bf16[1,2048,768]{2,1,0:T(8,128)(2,1)}, u32[]{:S(2)}) %copy-start.1) | copy-done | bytes 3145752
  91.8 2.4 %add_convert_fusion = bf16[1,2048,768]{2,1,0:T(8,128)(2,1)} fusion(f32[1,2048,768]{2,1,0:T(8,128)S(1)} %bitcast.28, bf16[1,2048,768]{2,1,0:T(8,128)(2,1)S(1)} %copy-done.1), kind=kLoop, calls=%fused_computation.4 | loop fusion | flops 4718592 | bytes 12582912 | tf_op jit(solution)/shard_map/convert_element_type | solution.py:51
  (6 shorter events, 0.1 us)
Async XLA Ops:
  0.6 2.1 %copy-start = (s32[32]{0:T(128)S(1)}, s32[32]{0:T(128)}, u32[]{:S(2)}) copy-start(s32[32]{0:T(128)} %param.14) | copy-start | bytes 388
  7.8 24.7 %all-to-all-start = ((bf16[32,2,768]{2,1,0:T(2,128)(2,1)}), bf16[32,2,768]{2,1,0:T(2,128)(2,1)S(1)}, u32[]{:S(2)}, u32[]{:S(2)}) async-start(bf16[32,2,768]{2,1,0:T(2,128)(2,1)} %gather_fusion.1), calls=%async_computation | async-start | bytes 196608 | tf_op jit(solution)/shard_map/all_to_all | solution.py:41
  89.9 1.9 %copy-start.1 = (bf16[1,2048,768]{2,1,0:T(8,128)(2,1)S(1)}, bf16[1,2048,768]{2,1,0:T(8,128)(2,1)}, u32[]{:S(2)}) copy-start(bf16[1,2048,768]{2,1,0:T(8,128)(2,1)} %param.15) | copy-start | bytes 9437188

commit v3 on v1

v3 whole, which is shorter than its diff:
```python
import jax
import jax.numpy as jnp
from jax import lax
from jax.experimental import pallas as pl
from jax.experimental.pallas import tpu as pltpu
from jax.sharding import Mesh
from jax.sharding import PartitionSpec as P

RING = 8
LIFT = 2.0**15
REPLICA = ("x_hi", "z")


def step_kernel(
    slot_ref,
    owner_ref,
    exponent_ref,
    master_ref,
    first_ref,
    second_ref,
    grad_ref,
    master_out_ref,
    first_out_ref,
    second_out_ref,
    sent_ref,
):
    slots, sub_rows, columns = master_ref.shape
    blocks = exponent_ref.shape[2]
    grad_full = grad_ref[...].astype(jnp.float32)
    first_out = 0.9 * first_ref[...] + 0.1 * grad_full
    second_out = 0.95 * second_ref[...] + 0.05 * grad_full * grad_full
    first_out_ref[...] = first_out
    second_out_ref[...] = second_out
    corr_first = 1.0 - 0.9**10
    corr_second = 1.0 - 0.95**10
    master = master_ref[...]
    update = first_out / corr_first / (jnp.sqrt(second_out / corr_second) + 1e-08) + 0.1 * master
    delta = -0.1 * update
    master_out_ref[...] = master + delta
    limit = 8.0 * jnp.exp2(-exponent_ref[...].astype(jnp.float32))
    width = columns // blocks
    limits = jnp.concatenate(
        [jnp.broadcast_to(limit[:, :, b : b + 1], (slots, sub_rows, width)) for b in range(blocks)],
        axis=2,
    )
    added = jnp.clip(delta, -limits, limits).astype(jnp.bfloat16)
    for slot in range(slots):
        owner = owner_ref[slot_ref[slot]]
        sent_ref[pl.ds(owner, 1)] = added[slot : slot + 1]


def shards(
    master,
    first_moment,
    second_moment,
    gradient,
    scale_exponent,
    slot_expert,
    expert_owner,
    serving_weights,
):
    state = jax.ShapeDtypeStruct(master.shape[2:], jnp.float32)
    wire_rows = jax.ShapeDtypeStruct(master.shape[2:], jnp.bfloat16)
    in_vmem = pl.BlockSpec(memory_space=pltpu.VMEM)
    in_smem = pl.BlockSpec(memory_space=pltpu.SMEM)
    master_out, first_out, second_out, sent = pl.pallas_call(
        step_kernel,
        in_specs=[in_smem, in_smem] + [in_vmem] * 5,
        out_specs=[in_vmem] * 4,
        out_shape=[state, state, state, wire_rows],
    )(
        slot_expert[0, 0],
        expert_owner,
        scale_exponent[0, 0],
        master[0, 0],
        first_moment[0, 0],
        second_moment[0, 0],
        gradient[0, 0],
    )
    received = lax.all_to_all(sent, "expert", split_axis=0, concat_axis=0, tiled=True)
    piece = received.reshape(-1, received.shape[2])
    part = lax.all_gather(piece, "x_hi", axis=0, tiled=False)
    wire = (part.astype(jnp.float32) * LIFT).astype(jnp.float16)
    whole = lax.all_gather(wire, "z", axis=1, tiled=True)
    serving = serving_weights.reshape(whole.shape)
    added = whole.astype(jnp.float32) * (1.0 / LIFT)
    new_rows = (serving.astype(jnp.float32) + added).astype(jnp.bfloat16)
    serving_out = new_rows.reshape(serving_weights.shape)
    return (master_out[None, None], first_out[None, None], second_out[None, None], serving_out)


def solution(mesh):
    replicas, experts = mesh.devices.shape
    split = Mesh(mesh.devices.reshape(replicas // RING, RING, experts), (*REPLICA, "expert"))
    flat = P(REPLICA, "expert", None, None, None)
    served = P("expert", None, None)
    in_specs = (flat, flat, flat, flat, flat, P(REPLICA, "expert", None), P(), served)
    out_specs = (flat, flat, flat, served)
    return jax.shard_map(shards, mesh=split, in_specs=in_specs, out_specs=out_specs, check_vma=False)
```

time: 154 us -> 89 us (0.58)
  the two profiles are of different devices: /device:TPU:16 before, /device:TPU:2 now
where the time goes in v3:
time: 89 us; the launch traced here: 88.8 us
  blocking collectives  81.2 us (91%)
  other arithmetic  2.85 us (3%)
  Pallas kernels  2.45 us (3%)
  local copies, waits for them, and re-layouts  1.58 us (2%)
    all_gather x1, blocking collectives, shards(): whole = lax.all_gather(wire, 'z', axis=1, tiled=True)  40.4 us
    all_to_all x1, blocking collectives, shards(): lax.all_to_all(sent, 'expert', split_axis=0, concat_axis=0, tiled=True)  24.7 us
    all_gather x1, blocking collectives, shards(): part = lax.all_gather(piece, 'x_hi', axis=0, tiled=False)  16.2 us
    convert_element_type x1, other arithmetic, shards(): new_rows = (serving.astype(jnp.float32) + added).astype(jnp.bfloat16)  2.76 us
    pallas_call x1, Pallas kernels, shards(): pl.pallas_call(step_kernel, in_specs=[in_smem, in_smem] + [in_vmem] * 5,...  2.45 us

profile of v3, /device:TPU:2, one launch (start us, length us, event | category | flops | bytes accessed | tf_op | source)
XLA Modules:
  0.0 88.8 jit_solution(7288825730525392492)
XLA Ops:
  0.6 0.0 copy-start
  0.6 1.5 %copy.13 = s32[1,1,32,2,6]{4,3,2,1,0:T(2,128)} copy(s32[1,1,32,2,6]{2,3,4,1,0:T(2,128)} %param.12) | data formatting | bytes 3072 | tf_op args[4]
  2.2 2.4 %shard_map.111 = (f32[32,2,768]{2,1,0:T(2,128)}, f32[32,2,768]{2,1,0:T(2,128)}, f32[32,2,768]{2,1,0:T(2,128)}, bf16[32,2,768]{2,1,0:T(2,128)(2,1)}) custom-call(s32[32]{0:T(128)} %bitcast.19, s32[32]{0:T(128)} %owner_ref.1, s32[32,2,6]{2,1,0:T(2,128)} %bitcast.17, f32[32,2,768]{2,1,0:T(2,128)} %bitcast.14, f32[32,2,768]{2,1,0:T(2,128)} %bitcast.15, ...), custom_call_target="tpu_custom_call" | custom-call | tf_op jit(solution)/shard_map/pallas_call | solution.py:66
  4.6 24.7 %all_to_all.5 = bf16[32,2,768]{2,1,0:T(2,128)(2,1)S(1)} all-to-all(bf16[32,2,768]{2,1,0:T(2,128)(2,1)} %get-tuple-element.11), channel_id=1, replica_groups=mesh['x_hi'=4,'z'=8,'expert'=32] {'expert'}, dimensions={0} | all-to-all | bytes 196608 | tf_op jit(solution)/shard_map/all_to_all | solution.py:80
  29.3 16.2 %all_gather.6 = bf16[4,64,768]{2,1,0:T(8,128)(2,1)S(1)} all-gather(bf16[1,64,768]{2,1,0:T(8,128)(2,1)S(1)} %all_gather_reshape.3), channel_id=1, replica_groups=mesh['x_hi'=4,'z'=8,'expert'=32] {'x_hi'}, dimensions={0}, use_global_device_ids=true | all-gather | bytes 491520 | tf_op jit(solution)/shard_map/all_gather | solution.py:82
  45.5 0.1 multiply_convert_fusion
  45.6 40.4 %all-gather.1 = f16[4,512,768]{2,1,0:T(8,128)(2,1)S(1)} all-gather(f16[4,64,768]{2,1,0:T(8,128)(2,1)S(1)} %multiply_convert_fusion), channel_id=1, replica_groups=mesh['x_hi'=4,'z'=8,'expert'=32] {'z'}, dimensions={1}, use_global_device_ids=true | all-gather | bytes 3538944 | tf_op jit(solution)/shard_map/all_gather | solution.py:84
  86.0 0.0 copy-done
  86.0 2.8 %fusion = bf16[4,512,768]{2,1,0:T(8,128)(2,1)} fusion(bf16[4,512,768]{2,1,0:T(8,128)(2,1)S(1)} %bitcast.12, f16[4,512,768]{2,1,0:T(8,128)(2,1)S(1)} %all-gather.1), kind=kLoop, calls=%fused_computation.1 | loop fusion | flops 7864320 | bytes 9437184 | tf_op jit(solution)/shard_map/convert_element_type | solution.py:87
  (1 shorter events, 0.0 us)
Async XLA Ops:
  0.6 85.4 %copy-start = (bf16[1,2048,768]{2,1,0:T(8,128)(2,1)S(1)}, bf16[1,2048,768]{2,1,0:T(8,128)(2,1)}, u32[]{:S(2)}) copy-start(bf16[1,2048,768]{2,1,0:T(8,128)(2,1)} %param.15) | copy-start | bytes 9437188

commit v4 on v3

v4 whole, which is shorter than its diff:
```python
import jax
import jax.numpy as jnp
from jax import lax
from jax.experimental import pallas as pl
from jax.experimental.pallas import tpu as pltpu
from jax.sharding import Mesh
from jax.sharding import PartitionSpec as P

RING = 8
CORES = 2
LIFT = 2.0**15
REPLICA = ("x_hi", "z")
EXPERT = ("tile", "core")


def step_kernel(
    slot_ref,
    owner_ref,
    exponent_ref,
    master_ref,
    first_ref,
    second_ref,
    grad_ref,
    master_out_ref,
    first_out_ref,
    second_out_ref,
    sent_ref,
):
    slots, sub_rows, columns = master_ref.shape
    blocks = exponent_ref.shape[0]
    grad_full = grad_ref[...].astype(jnp.float32)
    first_out = 0.9 * first_ref[...] + 0.1 * grad_full
    second_out = 0.95 * second_ref[...] + 0.05 * grad_full * grad_full
    first_out_ref[...] = first_out
    second_out_ref[...] = second_out
    corr_first = 1.0 - 0.9**10
    corr_second = 1.0 - 0.95**10
    master = master_ref[...]
    update = first_out / corr_first / (jnp.sqrt(second_out / corr_second) + 1e-08) + 0.1 * master
    delta = -0.1 * update
    master_out_ref[...] = master + delta
    limit = 8.0 * jnp.exp2(-exponent_ref[...].astype(jnp.float32))
    width = columns // blocks
    for slot in range(slots):
        limits = jnp.concatenate(
            [
                jnp.broadcast_to(limit[b, :, slot : slot + 1], (sub_rows, width))
                for b in range(blocks)
            ],
            axis=1,
        )
        added = jnp.clip(delta[slot], -limits, limits).astype(jnp.bfloat16)
        owner = owner_ref[slot_ref[slot]]
        place = lax.rem(owner, CORES) * (slots // CORES) + lax.div(owner, CORES)
        sent_ref[pl.ds(place, 1)] = added[None]


def shards(
    master,
    first_moment,
    second_moment,
    gradient,
    scale_exponent,
    slot_expert,
    expert_owner,
    serving_weights,
):
    slots, sub_rows, columns = master.shape[2:]
    state = jax.ShapeDtypeStruct((slots, sub_rows, columns), jnp.float32)
    wire_rows = jax.ShapeDtypeStruct((slots, sub_rows, columns), jnp.bfloat16)
    in_vmem = pl.BlockSpec(memory_space=pltpu.VMEM)
    in_smem = pl.BlockSpec(memory_space=pltpu.SMEM)
    master_out, first_out, second_out, sent = pl.pallas_call(
        step_kernel,
        in_specs=[in_smem, in_smem] + [in_vmem] * 5,
        out_specs=[in_vmem] * 4,
        out_shape=[state, state, state, wire_rows],
    )(
        slot_expert[0, 0],
        expert_owner,
        jnp.transpose(scale_exponent[0, 0], (2, 1, 0)),
        master[0, 0],
        first_moment[0, 0],
        second_moment[0, 0],
        gradient[0, 0],
    )
    on_core = lax.all_to_all(sent, "core", split_axis=0, concat_axis=0, tiled=True)
    tiles = slots // CORES
    by_tile = jnp.transpose(on_core.reshape(CORES, tiles, sub_rows, columns), (1, 0, 2, 3))
    copies = lax.axis_size("x_hi")
    blocks = jnp.broadcast_to(
        by_tile.reshape(1, tiles, CORES * sub_rows, columns),
        (copies, tiles, CORES * sub_rows, columns),
    ).reshape(copies * tiles, CORES * sub_rows, columns)
    received = lax.all_to_all(blocks, ("x_hi", "tile"), split_axis=0, concat_axis=0, tiled=True)
    part = received.reshape(copies, slots * sub_rows, columns)
    wire = (part.astype(jnp.float32) * LIFT).astype(jnp.float16)
    whole = lax.all_gather(wire, "z", axis=1, tiled=True)
    serving = serving_weights.reshape(whole.shape)
    added = whole.astype(jnp.float32) * (1.0 / LIFT)
    new_rows = (serving.astype(jnp.float32) + added).astype(jnp.bfloat16)
    serving_out = new_rows.reshape(serving_weights.shape)
    return (master_out[None, None], first_out[None, None], second_out[None, None], serving_out)


def solution(mesh):
    replicas, experts = mesh.devices.shape
    shape = (replicas // RING, RING, experts // CORES, CORES)
    split = Mesh(mesh.devices.reshape(shape), (*REPLICA, *EXPERT))
    flat = P(REPLICA, EXPERT, None, None, None)
    served = P(EXPERT, None, None)
    in_specs = (flat, flat, flat, flat, flat, P(REPLICA, EXPERT, None), P(), served)
    out_specs = (flat, flat, flat, served)
    return jax.shard_map(shards, mesh=split, in_specs=in_specs, out_specs=out_specs, check_vma=False)
```

time: 89 us -> 90.7 us (1.019)
  the two profiles are of different devices: /device:TPU:2 before, /device:TPU:4 now
where the time goes in v4:
time: 90.7 us; the launch traced here: 90.4 us
  blocking collectives  83.3 us (92%)
  other arithmetic  2.97 us (3%)
  Pallas kernels  2.42 us (3%)
  local copies, waits for them, and re-layouts  1.05 us (1%)
    all_gather x1, blocking collectives, shards(): whole = lax.all_gather(wire, 'z', axis=1, tiled=True)  44.6 us
    all_to_all x1, blocking collectives, shards(): lax.all_to_all(blocks, ('x_hi', 'tile'), split_axis=0, concat_axis=0, til...  34 us
    all_to_all x1, blocking collectives, shards(): lax.all_to_all(sent, 'core', split_axis=0, concat_axis=0, tiled=True)  4.76 us
    convert_element_type x1, other arithmetic, shards(): new_rows = (serving.astype(jnp.float32) + added).astype(jnp.bfloat16)  2.76 us
    pallas_call x1, Pallas kernels, shards(): pl.pallas_call(step_kernel, in_specs=[in_smem, in_smem] + [in_vmem] * 5,...  2.42 us

profile of v4, /device:TPU:4, one launch (start us, length us, event | category | flops | bytes accessed | tf_op | source)
XLA Modules:
  0.0 90.4 jit_solution(12986834444972801406)
XLA Ops:
  0.6 2.4 %shard_map.111 = (f32[32,2,768]{2,1,0:T(2,128)}, f32[32,2,768]{2,1,0:T(2,128)}, f32[32,2,768]{2,1,0:T(2,128)}, bf16[32,2,768]{2,1,0:T(2,128)(2,1)}) custom-call(s32[32]{0:T(128)} %bitcast.29, s32[32]{0:T(128)} %owner_ref.1, s32[6,2,32]{2,1,0:T(2,128)} %bitcast.28, f32[32,2,768]{2,1,0:T(2,128)} %bitcast.24, f32[32,2,768]{2,1,0:T(2,128)} %bitcast.25, ...), custom_call_target="tpu_custom_call" | custom-call | tf_op jit(solution)/shard_map/pallas_call | solution.py:73
  3.0 4.8 %all_to_all.10 = bf16[32,2,768]{2,1,0:T(2,128)(2,1)S(1)} all-to-all(bf16[32,2,768]{2,1,0:T(2,128)(2,1)} %get-tuple-element.11), channel_id=1, replica_groups=mesh['x_hi'=4,'z'=8,'tile'=16,'core'=2] {'core'}, dimensions={0} | all-to-all | bytes 196608 | tf_op jit(solution)/shard_map/all_to_all | solution.py:87
  7.8 0.1 copy.13
  7.9 0.0 copy-start
  7.9 0.1 broadcast_in_dim.20
  8.0 34.0 %all_to_all.11 = bf16[64,4,768]{2,1,0:T(4,128)(2,1)S(1)} all-to-all(bf16[64,4,768]{2,1,0:T(4,128)(2,1)S(1)} %bitcast.21), channel_id=1, replica_groups=mesh['x_hi'=4,'z'=8,'tile'=16,'core'=2] {'x_hi','tile'}, dimensions={0} | all-to-all | bytes 786432 | tf_op jit(solution)/shard_map/all_to_all | solution.py:95
  42.0 0.2 multiply_convert_fusion
  42.2 0.9 convert_element_type.26
  43.1 44.6 %all-gather.1 = f16[4,512,768]{2,1,0:T(8,128)(2,1)S(1)} all-gather(f16[4,64,768]{2,1,0:T(8,128)(2,1)} %convert_element_type.26), channel_id=1, replica_groups=mesh['x_hi'=4,'z'=8,'tile'=16,'core'=2] {'z'}, dimensions={1}, use_global_device_ids=true | all-gather | bytes 3538944 | tf_op jit(solution)/shard_map/all_gather | solution.py:98
  87.6 0.0 copy-done
  87.6 2.8 %fusion = bf16[4,512,768]{2,1,0:T(8,128)(2,1)} fusion(bf16[4,512,768]{2,1,0:T(8,128)(2,1)S(1)} %bitcast.19, f16[4,512,768]{2,1,0:T(8,128)(2,1)S(1)} %all-gather.1), kind=kLoop, calls=%fused_computation.1 | loop fusion | flops 7864320 | bytes 9437184 | tf_op jit(solution)/shard_map/convert_element_type | solution.py:101
  (1 shorter events, 0.0 us)
Async XLA Ops:
  7.9 79.8 %copy-start = (bf16[1,2048,768]{2,1,0:T(8,128)(2,1)S(1)}, bf16[1,2048,768]{2,1,0:T(8,128)(2,1)}, u32[]{:S(2)}) copy-start(bf16[1,2048,768]{2,1,0:T(8,128)(2,1)} %param.15) | copy-start | bytes 9437188

commit v5 on v3

--- a/solution.py
+++ b/solution.py
@@ -25,7 +25,7 @@
     sent_ref,
 ):
     slots, sub_rows, columns = master_ref.shape
-    blocks = exponent_ref.shape[2]
+    blocks = exponent_ref.shape[0]
     grad_full = grad_ref[...].astype(jnp.float32)
     first_out = 0.9 * first_ref[...] + 0.1 * grad_full
     second_out = 0.95 * second_ref[...] + 0.05 * grad_full * grad_full
@@ -39,14 +39,16 @@
     master_out_ref[...] = master + delta
     limit = 8.0 * jnp.exp2(-exponent_ref[...].astype(jnp.float32))
     width = columns // blocks
-    limits = jnp.concatenate(
-        [jnp.broadcast_to(limit[:, :, b : b + 1], (slots, sub_rows, width)) for b in range(blocks)],
-        axis=2,
-    )
-    added = jnp.clip(delta, -limits, limits).astype(jnp.bfloat16)
     for slot in range(slots):
-        owner = owner_ref[slot_ref[slot]]
-        sent_ref[pl.ds(owner, 1)] = added[slot : slot + 1]
+        limits = jnp.concatenate(
+            [
+                jnp.broadcast_to(limit[b, :, slot : slot + 1], (sub_rows, width))
+                for b in range(blocks)
+            ],
+            axis=1,
+        )
+        added = jnp.clip(delta[slot], -limits, limits).astype(jnp.bfloat16)
+        sent_ref[pl.ds(owner_ref[slot_ref[slot]], 1)] = added[None]
 
 
 def shards(
@@ -71,7 +73,7 @@
     )(
         slot_expert[0, 0],
         expert_owner,
-        scale_exponent[0, 0],
+        jnp.transpose(scale_exponent[0, 0], (2, 1, 0)),
         master[0, 0],
         first_moment[0, 0],
         second_moment[0, 0],

time: 89 us -> 87.5 us (0.983)
  local copies, waits for them, and re-layouts: 1.58 us -> 0.04 us
    unnamed x3 -> x2, local copies, waits for them, and re-layouts: 1.54 us -> 0.01 us
where the time goes in v5:
time: 87.5 us; the launch traced here: 87.3 us
  blocking collectives  81.2 us (93%)
  other arithmetic  2.85 us (3%)
  Pallas kernels  2.56 us (3%)
    all_gather x1, blocking collectives, shards(): whole = lax.all_gather(wire, 'z', axis=1, tiled=True)  40.4 us
    all_to_all x1, blocking collectives, shards(): lax.all_to_all(sent, 'expert', split_axis=0, concat_axis=0, tiled=True)  24.7 us
    all_gather x1, blocking collectives, shards(): part = lax.all_gather(piece, 'x_hi', axis=0, tiled=False)  16.2 us
    convert_element_type x1, other arithmetic, shards(): new_rows = (serving.astype(jnp.float32) + added).astype(jnp.bfloat16)  2.76 us
    pallas_call x1, Pallas kernels, shards(): pl.pallas_call(step_kernel, in_specs=[in_smem, in_smem] + [in_vmem] * 5,...  2.56 us

profile of v5, /device:TPU:2, one launch (start us, length us, event | category | flops | bytes accessed | tf_op | source)
XLA Modules:
  0.0 87.3 jit_solution(11621774486726932764)
XLA Ops:
  0.6 0.0 copy-start
  0.6 2.6 %shard_map.111 = (f32[32,2,768]{2,1,0:T(2,128)}, f32[32,2,768]{2,1,0:T(2,128)}, f32[32,2,768]{2,1,0:T(2,128)}, bf16[32,2,768]{2,1,0:T(2,128)(2,1)}) custom-call(s32[32]{0:T(128)} %bitcast.21, s32[32]{0:T(128)} %owner_ref.1, s32[6,2,32]{2,1,0:T(2,128)} %bitcast.20, f32[32,2,768]{2,1,0:T(2,128)} %bitcast.16, f32[32,2,768]{2,1,0:T(2,128)} %bitcast.17, ...), custom_call_target="tpu_custom_call" | custom-call | tf_op jit(solution)/shard_map/pallas_call | solution.py:68
  3.2 24.7 %all_to_all.5 = bf16[32,2,768]{2,1,0:T(2,128)(2,1)S(1)} all-to-all(bf16[32,2,768]{2,1,0:T(2,128)(2,1)} %get-tuple-element.11), channel_id=1, replica_groups=mesh['x_hi'=4,'z'=8,'expert'=32] {'expert'}, dimensions={0} | all-to-all | bytes 196608 | tf_op jit(solution)/shard_map/all_to_all | solution.py:82
  27.9 16.2 %all_gather.6 = bf16[4,64,768]{2,1,0:T(8,128)(2,1)S(1)} all-gather(bf16[1,64,768]{2,1,0:T(8,128)(2,1)S(1)} %all_gather_reshape.3), channel_id=1, replica_groups=mesh['x_hi'=4,'z'=8,'expert'=32] {'x_hi'}, dimensions={0}, use_global_device_ids=true | all-gather | bytes 491520 | tf_op jit(solution)/shard_map/all_gather | solution.py:84
  44.1 0.1 multiply_convert_fusion
  44.2 40.4 %all-gather.1 = f16[4,512,768]{2,1,0:T(8,128)(2,1)S(1)} all-gather(f16[4,64,768]{2,1,0:T(8,128)(2,1)S(1)} %multiply_convert_fusion), channel_id=1, replica_groups=mesh['x_hi'=4,'z'=8,'expert'=32] {'z'}, dimensions={1}, use_global_device_ids=true | all-gather | bytes 3538944 | tf_op jit(solution)/shard_map/all_gather | solution.py:86
  84.6 0.0 copy-done
  84.6 2.8 %fusion = bf16[4,512,768]{2,1,0:T(8,128)(2,1)} fusion(bf16[4,512,768]{2,1,0:T(8,128)(2,1)S(1)} %bitcast.14, f16[4,512,768]{2,1,0:T(8,128)(2,1)S(1)} %all-gather.1), kind=kLoop, calls=%fused_computation.1 | loop fusion | flops 7864320 | bytes 9437184 | tf_op jit(solution)/shard_map/convert_element_type | solution.py:89
  (1 shorter events, 0.0 us)
Async XLA Ops:
  0.6 83.9 %copy-start = (bf16[1,2048,768]{2,1,0:T(8,128)(2,1)S(1)}, bf16[1,2048,768]{2,1,0:T(8,128)(2,1)}, u32[]{:S(2)}) copy-start(bf16[1,2048,768]{2,1,0:T(8,128)(2,1)} %param.15) | copy-start | bytes 9437188

commit v6 on v5

--- a/solution.py
+++ b/solution.py
@@ -11,7 +11,17 @@
 REPLICA = ("x_hi", "z")
 
 
-def step_kernel(
+def adamw(master, first_moment, second_moment, gradient):
+    grad_full = gradient.astype(jnp.float32)
+    first_out = 0.9 * first_moment + 0.1 * grad_full
+    second_out = 0.95 * second_moment + 0.05 * grad_full * grad_full
+    corr_first = 1.0 - 0.9**10
+    corr_second = 1.0 - 0.95**10
+    update = first_out / corr_first / (jnp.sqrt(second_out / corr_second) + 1e-08) + 0.1 * master
+    return first_out, second_out, -0.1 * update
+
+
+def coded_kernel(
     slot_ref,
     owner_ref,
     exponent_ref,
@@ -19,24 +29,11 @@
     first_ref,
     second_ref,
     grad_ref,
-    master_out_ref,
-    first_out_ref,
-    second_out_ref,
     sent_ref,
 ):
     slots, sub_rows, columns = master_ref.shape
     blocks = exponent_ref.shape[0]
-    grad_full = grad_ref[...].astype(jnp.float32)
-    first_out = 0.9 * first_ref[...] + 0.1 * grad_full
-    second_out = 0.95 * second_ref[...] + 0.05 * grad_full * grad_full
-    first_out_ref[...] = first_out
-    second_out_ref[...] = second_out
-    corr_first = 1.0 - 0.9**10
-    corr_second = 1.0 - 0.95**10
-    master = master_ref[...]
-    update = first_out / corr_first / (jnp.sqrt(second_out / corr_second) + 1e-08) + 0.1 * master
-    delta = -0.1 * update
-    master_out_ref[...] = master + delta
+    _, _, delta = adamw(master_ref[...], first_ref[...], second_ref[...], grad_ref[...])
     limit = 8.0 * jnp.exp2(-exponent_ref[...].astype(jnp.float32))
     width = columns // blocks
     for slot in range(slots):
@@ -61,15 +58,13 @@
     expert_owner,
     serving_weights,
 ):
-    state = jax.ShapeDtypeStruct(master.shape[2:], jnp.float32)
-    wire_rows = jax.ShapeDtypeStruct(master.shape[2:], jnp.bfloat16)
     in_vmem = pl.BlockSpec(memory_space=pltpu.VMEM)
     in_smem = pl.BlockSpec(memory_space=pltpu.SMEM)
-    master_out, first_out, second_out, sent = pl.pallas_call(
-        step_kernel,
+    sent = pl.pallas_call(
+        coded_kernel,
         in_specs=[in_smem, in_smem] + [in_vmem] * 5,
-        out_specs=[in_vmem] * 4,
-        out_shape=[state, state, state, wire_rows],
+        out_specs=in_vmem,
+        out_shape=jax.ShapeDtypeStruct(master.shape[2:], jnp.bfloat16),
     )(
         slot_expert[0, 0],
         expert_owner,
@@ -80,6 +75,8 @@
         gradient[0, 0],
     )
     received = lax.all_to_all(sent, "expert", split_axis=0, concat_axis=0, tiled=True)
+    first_out, second_out, delta = adamw(master, first_moment, second_moment, gradient)
+    master_out = master + delta
     piece = received.reshape(-1, received.shape[2])
     part = lax.all_gather(piece, "x_hi", axis=0, tiled=False)
     wire = (part.astype(jnp.float32) * LIFT).astype(jnp.float16)
@@ -88,7 +85,7 @@
     added = whole.astype(jnp.float32) * (1.0 / LIFT)
     new_rows = (serving.astype(jnp.float32) + added).astype(jnp.bfloat16)
     serving_out = new_rows.reshape(serving_weights.shape)
-    return (master_out[None, None], first_out[None, None], second_out[None, None], serving_out)
+    return (master_out, first_out, second_out, serving_out)
 
 
 def solution(mesh):

time: 87.5 us -> 87.2 us (level)
  blocking collectives: 81.2 us -> 56.6 us
  starting transfers between devices: 0 us -> 16.8 us
  waiting for transfers between devices: 0 us -> 5.13 us
  other arithmetic: 2.85 us -> 5.62 us
    all_to_all x1 -> x0, blocking collectives: 24.7 us -> none  [shards(): lax.all_to_all(sent, 'expert', split_axis=0, concat_axis=0, tiled=True)]
    all_to_all x0 -> x1, starting transfers between devices: none -> 16.8 us  [shards(): lax.all_to_all(sent, 'expert', split_axis=0, concat_axis=0, tiled=True)]
    all_to_all x0 -> x1, waiting for transfers between devices: none -> 5.13 us  [shards(): lax.all_to_all(sent, 'expert', split_axis=0, concat_axis=0, tiled=True)]
    add x0 -> x1, other arithmetic: none -> 2.77 us  [shards(): master_out = master + delta]
  transfers between devices with their start and end apart: 0 -> 1, of which waited for: 0 -> 1; matrix products, arithmetic and copies ran while one was open for 0% -> 3% of each run, Pallas kernels for 0% -> 0%
where the time goes in v6:
time: 87.2 us; the launch traced here: 87 us
  blocking collectives  56.6 us (65%)
  starting transfers between devices  16.8 us (19%)
  other arithmetic  5.62 us (6%)
  waiting for transfers between devices  5.13 us (6%)
  Pallas kernels  2.24 us (3%)
    all_gather x1, blocking collectives, shards(): whole = lax.all_gather(wire, 'z', axis=1, tiled=True)  40.4 us
    all_to_all x1, starting transfers between devices, shards(): lax.all_to_all(sent, 'expert', split_axis=0, concat_axis=0, tiled=True)  16.8 us
    all_gather x1, blocking collectives, shards(): part = lax.all_gather(piece, 'x_hi', axis=0, tiled=False)  16.2 us
    all_to_all x1, waiting for transfers between devices, shards(): lax.all_to_all(sent, 'expert', split_axis=0, concat_axis=0, tiled=True)  5.13 us
    add x1, other arithmetic, shards(): master_out = master + delta  2.77 us
    convert_element_type x1, other arithmetic, shards(): new_rows = (serving.astype(jnp.float32) + added).astype(jnp.bfloat16)  2.76 us
    pallas_call x1, Pallas kernels, shards(): pl.pallas_call(coded_kernel, in_specs=[in_smem, in_smem] + [in_vmem] * 5,...  2.24 us
  transfers between devices with their start and end apart: 1, of which 1 were waited for; matrix products, arithmetic and copies ran while one was open for 3% of the time, Pallas kernels for 0%

profile of v6, /device:TPU:2, one launch (start us, length us, event | category | flops | bytes accessed | tf_op | source)
XLA Modules:
  0.0 87.0 jit_solution(6345757172927667686)
XLA Ops:
  0.6 2.2 %shard_map.111 = bf16[32,2,768]{2,1,0:T(2,128)(2,1)} custom-call(s32[32]{0:T(128)} %bitcast.18, s32[32]{0:T(128)} %owner_ref.1, s32[6,2,32]{2,1,0:T(2,128)} %bitcast.17, f32[32,2,768]{2,1,0:T(2,128)} %bitcast.13, f32[32,2,768]{2,1,0:T(2,128)} %bitcast.14, f32[32,2,768]{2,1,0:T(2,128)} %bitcast.15, bf16[32,2,768]{2,1,0:T(2,128)(2,1)} %bitcast.16), custom_call_target="tpu_custom_call" | custom-call | tf_op jit(solution)/shard_map/pallas_call | solution.py:63
  2.9 16.8 %all-to-all-start = ((bf16[32,2,768]{2,1,0:T(2,128)(2,1)}), bf16[32,2,768]{2,1,0:T(2,128)(2,1)S(1)}, u32[]{:S(2)}, u32[]{:S(2)}) async-start(bf16[32,2,768]{2,1,0:T(2,128)(2,1)} %shard_map.111), calls=%async_computation | async-start | bytes 196608 | tf_op jit(solution)/shard_map/all_to_all | solution.py:77
  19.6 0.0 copy-start
  19.7 2.8 %multiply_add_fusion = (f32[1,1,32,2,768]{4,3,2,1,0:T(2,128)}, f32[1,1,32,2,768]{4,3,2,1,0:T(2,128)}, f32[1,1,32,2,768]{4,3,2,1,0:T(2,128)}) fusion(f32[1,1,32,2,768]{4,3,2,1,0:T(2,128)} %param.8, bf16[1,1,32,2,768]{4,3,2,1,0:T(2,128)(2,1)} %param.11, f32[1,1,32,2,768]{4,3,2,1,0:T(2,128)} %param.9, f32[1,1,32,2,768]{4,3,2,1,0:T(2,128)} %param.10), kind=kLoop, calls=%fused_computation.7 | loop fusion | flops 786432 | bytes 1277952 | tf_op jit(solution)/shard_map/add | solution.py:79
  22.4 5.1 %all-to-all-done = bf16[32,2,768]{2,1,0:T(2,128)(2,1)S(1)} async-done(((bf16[32,2,768]{2,1,0:T(2,128)(2,1)}), bf16[32,2,768]{2,1,0:T(2,128)(2,1)S(1)}, u32[]{:S(2)}, u32[]{:S(2)}) %all-to-all-start) | async-done | bytes 98336 | tf_op jit(solution)/shard_map/all_to_all | solution.py:77
  27.6 16.2 %all_gather.6 = bf16[4,64,768]{2,1,0:T(8,128)(2,1)S(1)} all-gather(bf16[1,64,768]{2,1,0:T(8,128)(2,1)S(1)} %all_gather_reshape.3), channel_id=1, replica_groups=mesh['x_hi'=4,'z'=8,'expert'=32] {'x_hi'}, dimensions={0}, use_global_device_ids=true | all-gather | bytes 491520 | tf_op jit(solution)/shard_map/all_gather | solution.py:81
  43.8 0.1 multiply_convert_fusion
  43.9 40.4 %all-gather.1 = f16[4,512,768]{2,1,0:T(8,128)(2,1)S(1)} all-gather(f16[4,64,768]{2,1,0:T(8,128)(2,1)S(1)} %multiply_convert_fusion), channel_id=1, replica_groups=mesh['x_hi'=4,'z'=8,'expert'=32] {'z'}, dimensions={1}, use_global_device_ids=true | all-gather | bytes 3538944 | tf_op jit(solution)/shard_map/all_gather | solution.py:83
  84.3 0.0 copy-done
  84.3 2.8 %fusion = bf16[4,512,768]{2,1,0:T(8,128)(2,1)} fusion(bf16[4,512,768]{2,1,0:T(8,128)(2,1)S(1)} %bitcast.11, f16[4,512,768]{2,1,0:T(8,128)(2,1)S(1)} %all-gather.1), kind=kLoop, calls=%fused_computation.1 | loop fusion | flops 7864320 | bytes 9437184 | tf_op jit(solution)/shard_map/convert_element_type | solution.py:86
  (1 shorter events, 0.0 us)
Async XLA Ops:
  2.9 24.7 %all-to-all-start = ((bf16[32,2,768]{2,1,0:T(2,128)(2,1)}), bf16[32,2,768]{2,1,0:T(2,128)(2,1)S(1)}, u32[]{:S(2)}, u32[]{:S(2)}) async-start(bf16[32,2,768]{2,1,0:T(2,128)(2,1)} %shard_map.111), calls=%async_computation | async-start | bytes 196608 | tf_op jit(solution)/shard_map/all_to_all | solution.py:77
  19.6 64.6 %copy-start = (bf16[1,2048,768]{2,1,0:T(8,128)(2,1)S(1)}, bf16[1,2048,768]{2,1,0:T(8,128)(2,1)}, u32[]{:S(2)}) copy-start(bf16[1,2048,768]{2,1,0:T(8,128)(2,1)} %param.15) | copy-start | bytes 9437188

commit v7 on v6

--- a/solution.py
+++ b/solution.py
@@ -78,7 +78,8 @@
     first_out, second_out, delta = adamw(master, first_moment, second_moment, gradient)
     master_out = master + delta
     piece = received.reshape(-1, received.shape[2])
-    part = lax.all_gather(piece, "x_hi", axis=0, tiled=False)
+    copies = jnp.broadcast_to(piece[None], (lax.axis_size("x_hi"), *piece.shape))
+    part = lax.all_to_all(copies, "x_hi", split_axis=0, concat_axis=0, tiled=True)
     wire = (part.astype(jnp.float32) * LIFT).astype(jnp.float16)
     whole = lax.all_gather(wire, "z", axis=1, tiled=True)
     serving = serving_weights.reshape(whole.shape)

time: 87.2 us -> 92 us (1.055)
  starting transfers between devices: 16.8 us -> 3.72 us
  blocking collectives: 56.6 us -> 67.6 us
  waiting for transfers between devices: 5.13 us -> 11.3 us
    all_to_all x0 -> x1, blocking collectives: none -> 24.7 us  [shards(): lax.all_to_all(sent, 'expert', split_axis=0, concat_axis=0, tiled=True)]
    all_gather x1 -> x0, blocking collectives: 16.2 us -> none  [shards(): part = lax.all_gather(piece, 'x_hi', axis=0, tiled=False)]
    all_to_all x1, starting transfers between devices: 16.8 us -> 3.72 us  [shards(): lax.all_to_all(copies, 'x_hi', split_axis=0, concat_axis=0, tiled=True)]
    all_to_all x1, waiting for transfers between devices: 5.13 us -> 11.3 us  [shards(): lax.all_to_all(copies, 'x_hi', split_axis=0, concat_axis=0, tiled=True)]
    all_gather x1, blocking collectives: 40.4 us -> 42.9 us  [shards(): whole = lax.all_gather(wire, 'z', axis=1, tiled=True)]
where the time goes in v7:
time: 92 us; the launch traced here: 91.8 us
  blocking collectives  67.6 us (73%)
  waiting for transfers between devices  11.3 us (12%)
  other arithmetic  5.47 us (6%)
  starting transfers between devices  3.72 us (4%)
  Pallas kernels  2.24 us (2%)
    all_gather x1, blocking collectives, shards(): whole = lax.all_gather(wire, 'z', axis=1, tiled=True)  42.9 us
    all_to_all x1, blocking collectives, shards(): lax.all_to_all(sent, 'expert', split_axis=0, concat_axis=0, tiled=True)  24.7 us
    all_to_all x1, waiting for transfers between devices, shards(): lax.all_to_all(copies, 'x_hi', split_axis=0, concat_axis=0, tiled=True)  11.3 us
    all_to_all x1, starting transfers between devices, shards(): lax.all_to_all(copies, 'x_hi', split_axis=0, concat_axis=0, tiled=True)  3.72 us
    convert_element_type x1, other arithmetic, shards(): new_rows = (serving.astype(jnp.float32) + added).astype(jnp.bfloat16)  2.76 us
    add x1, other arithmetic, shards(): master_out = master + delta  2.62 us
    pallas_call x1, Pallas kernels, shards(): pl.pallas_call(coded_kernel, in_specs=[in_smem, in_smem] + [in_vmem] * 5,...  2.24 us
  transfers between devices with their start and end apart: 1, of which 1 were waited for; matrix products, arithmetic and copies ran while one was open for 3% of the time, Pallas kernels for 0%

profile of v7, /device:TPU:2, one launch (start us, length us, event | category | flops | bytes accessed | tf_op | source)
XLA Modules:
  0.0 91.8 jit_solution(1553346491109021089)
XLA Ops:
  0.6 2.2 %shard_map.111 = bf16[32,2,768]{2,1,0:T(2,128)(2,1)} custom-call(s32[32]{0:T(128)} %bitcast.18, s32[32]{0:T(128)} %owner_ref.1, s32[6,2,32]{2,1,0:T(2,128)} %bitcast.17, f32[32,2,768]{2,1,0:T(2,128)} %bitcast.13, f32[32,2,768]{2,1,0:T(2,128)} %bitcast.14, f32[32,2,768]{2,1,0:T(2,128)} %bitcast.15, bf16[32,2,768]{2,1,0:T(2,128)(2,1)} %bitcast.16), custom_call_target="tpu_custom_call" | custom-call | tf_op jit(solution)/shard_map/pallas_call | solution.py:63
  2.9 24.7 %all_to_all.10 = bf16[32,2,768]{2,1,0:T(2,128)(2,1)S(1)} all-to-all(bf16[32,2,768]{2,1,0:T(2,128)(2,1)} %shard_map.111), channel_id=1, replica_groups=mesh['x_hi'=4,'z'=8,'expert'=32] {'expert'}, dimensions={0} | all-to-all | bytes 196608 | tf_op jit(solution)/shard_map/all_to_all | solution.py:77
  27.6 0.8 broadcast_in_dim.8
  28.4 0.0 copy-start
  28.4 3.7 %all-to-all-start.1 = ((bf16[4,64,768]{2,1,0:T(8,128)(2,1)}), bf16[4,64,768]{2,1,0:T(8,128)(2,1)S(1)}, u32[]{:S(2)}, u32[]{:S(2)}) async-start(bf16[4,64,768]{2,1,0:T(8,128)(2,1)} %broadcast_in_dim.8), calls=%async_computation.1 | async-start | bytes 786432 | tf_op jit(solution)/shard_map/all_to_all | solution.py:82
  32.1 2.6 %multiply_add_fusion = (f32[1,1,32,2,768]{4,3,2,1,0:T(2,128)}, f32[1,1,32,2,768]{4,3,2,1,0:T(2,128)}, f32[1,1,32,2,768]{4,3,2,1,0:T(2,128)}) fusion(f32[1,1,32,2,768]{4,3,2,1,0:T(2,128)} %param.8, bf16[1,1,32,2,768]{4,3,2,1,0:T(2,128)(2,1)} %param.11, f32[1,1,32,2,768]{4,3,2,1,0:T(2,128)} %param.9, f32[1,1,32,2,768]{4,3,2,1,0:T(2,128)} %param.10), kind=kLoop, calls=%fused_computation.7 | loop fusion | flops 786432 | bytes 1277952 | tf_op jit(solution)/shard_map/add | solution.py:79
  34.7 11.3 %all-to-all-done.1 = bf16[4,64,768]{2,1,0:T(8,128)(2,1)S(1)} async-done(((bf16[4,64,768]{2,1,0:T(8,128)(2,1)}), bf16[4,64,768]{2,1,0:T(8,128)(2,1)S(1)}, u32[]{:S(2)}, u32[]{:S(2)}) %all-to-all-start.1) | async-done | bytes 393248 | tf_op jit(solution)/shard_map/all_to_all | solution.py:82
  46.0 0.1 multiply_convert_fusion
  46.1 42.9 %all-gather.1 = f16[4,512,768]{2,1,0:T(8,128)(2,1)S(1)} all-gather(f16[4,64,768]{2,1,0:T(8,128)(2,1)S(1)} %multiply_convert_fusion), channel_id=1, replica_groups=mesh['x_hi'=4,'z'=8,'expert'=32] {'z'}, dimensions={1}, use_global_device_ids=true | all-gather | bytes 3538944 | tf_op jit(solution)/shard_map/all_gather | solution.py:84
  89.0 0.0 copy-done
  89.0 2.8 %fusion = bf16[4,512,768]{2,1,0:T(8,128)(2,1)} fusion(bf16[4,512,768]{2,1,0:T(8,128)(2,1)S(1)} %bitcast.11, f16[4,512,768]{2,1,0:T(8,128)(2,1)S(1)} %all-gather.1), kind=kLoop, calls=%fused_computation.1 | loop fusion | flops 7864320 | bytes 9437184 | tf_op jit(solution)/shard_map/convert_element_type | solution.py:87
  (1 shorter events, 0.0 us)
Async XLA Ops:
  28.4 60.6 %copy-start = (bf16[1,2048,768]{2,1,0:T(8,128)(2,1)S(1)}, bf16[1,2048,768]{2,1,0:T(8,128)(2,1)}, u32[]{:S(2)}) copy-start(bf16[1,2048,768]{2,1,0:T(8,128)(2,1)} %param.15) | copy-start | bytes 9437188
  28.4 17.6 %all-to-all-start.1 = ((bf16[4,64,768]{2,1,0:T(8,128)(2,1)}), bf16[4,64,768]{2,1,0:T(8,128)(2,1)S(1)}, u32[]{:S(2)}, u32[]{:S(2)}) async-start(bf16[4,64,768]{2,1,0:T(8,128)(2,1)} %broadcast_in_dim.8), calls=%async_computation.1 | async-start | bytes 786432 | tf_op jit(solution)/shard_map/all_to_all | solution.py:82

commit v8 on v6

--- a/solution.py
+++ b/solution.py
@@ -8,6 +8,8 @@
 
 RING = 8
 LIFT = 2.0**15
+PIECES = 8
+GRANT = 8 * 2**20
 REPLICA = ("x_hi", "z")
 
 
@@ -48,6 +50,17 @@
         sent_ref[pl.ds(owner_ref[slot_ref[slot]], 1)] = added[None]
 
 
+def write_kernel(new_ref, out_ref, done_ref):
+    step = new_ref.shape[0] // PIECES
+    copies = []
+    for piece in range(PIECES):
+        rows = pl.ds(piece * step, step)
+        copies.append(pltpu.make_async_copy(new_ref.at[rows], out_ref.at[rows], done_ref.at[piece]))
+        copies[-1].start()
+    for copy in copies:
+        copy.wait()
+
+
 def shards(
     master,
     first_moment,
@@ -84,7 +97,15 @@
     serving = serving_weights.reshape(whole.shape)
     added = whole.astype(jnp.float32) * (1.0 / LIFT)
     new_rows = (serving.astype(jnp.float32) + added).astype(jnp.bfloat16)
-    serving_out = new_rows.reshape(serving_weights.shape)
+    new_rows = pltpu.with_memory_space_constraint(new_rows.reshape(serving_weights.shape[1:]), pltpu.VMEM)
+    serving_out = pl.pallas_call(
+        write_kernel,
+        in_specs=[in_vmem],
+        out_specs=pl.BlockSpec(memory_space=pl.ANY),
+        out_shape=jax.ShapeDtypeStruct(new_rows.shape, jnp.bfloat16),
+        scratch_shapes=[pltpu.SemaphoreType.DMA((PIECES,))],
+        compiler_params=pltpu.CompilerParams(vmem_limit_bytes=GRANT),
+    )(new_rows)[None]
     return (master_out, first_out, second_out, serving_out)
 
 

time: 87.2 us -> 87.3 us (level)
  Pallas kernels: 2.24 us -> 3.96 us
  other arithmetic: 5.62 us -> 3.98 us
    pallas_call x0 -> x1, Pallas kernels: none -> 1.72 us  [shards(): pl.pallas_call(write_kernel, in_specs=[in_vmem], out_specs=pl.BlockSpec(m...]
    convert_element_type x1, other arithmetic: 2.76 us -> 1.12 us  [shards(): new_rows = (serving.astype(jnp.float32) + added).astype(jnp.bfloat16)]
where the time goes in v8:
time: 87.3 us; the launch traced here: 87.1 us
  blocking collectives  56.6 us (65%)
  starting transfers between devices  16.8 us (19%)
  waiting for transfers between devices  5.13 us (6%)
  other arithmetic  3.98 us (5%)
  Pallas kernels  3.96 us (5%)
    all_gather x1, blocking collectives, shards(): whole = lax.all_gather(wire, 'z', axis=1, tiled=True)  40.4 us
    all_to_all x1, starting transfers between devices, shards(): lax.all_to_all(sent, 'expert', split_axis=0, concat_axis=0, tiled=True)  16.8 us
    all_gather x1, blocking collectives, shards(): part = lax.all_gather(piece, 'x_hi', axis=0, tiled=False)  16.2 us
    all_to_all x1, waiting for transfers between devices, shards(): lax.all_to_all(sent, 'expert', split_axis=0, concat_axis=0, tiled=True)  5.13 us
    add x1, other arithmetic, shards(): master_out = master + delta  2.77 us
    pallas_call x1, Pallas kernels, shards(): pl.pallas_call(coded_kernel, in_specs=[in_smem, in_smem] + [in_vmem] * 5,...  2.24 us
  transfers between devices with their start and end apart: 1, of which 1 were waited for; matrix products, arithmetic and copies ran while one was open for 3% of the time, Pallas kernels for 0%

profile of v8, /device:TPU:2, one launch (start us, length us, event | category | flops | bytes accessed | tf_op | source)
XLA Modules:
  0.0 87.1 jit_solution(17550955357635497859)
XLA Ops:
  0.6 2.2 %shard_map.111 = bf16[32,2,768]{2,1,0:T(2,128)(2,1)} custom-call(s32[32]{0:T(128)} %bitcast.20, s32[32]{0:T(128)} %owner_ref.1, s32[6,2,32]{2,1,0:T(2,128)} %bitcast.19, f32[32,2,768]{2,1,0:T(2,128)} %bitcast.15, f32[32,2,768]{2,1,0:T(2,128)} %bitcast.16, f32[32,2,768]{2,1,0:T(2,128)} %bitcast.17, bf16[32,2,768]{2,1,0:T(2,128)(2,1)} %bitcast.18), custom_call_target="tpu_custom_call" | custom-call | tf_op jit(solution)/shard_map/pallas_call | solution.py:76
  2.9 16.8 %all-to-all-start = ((bf16[32,2,768]{2,1,0:T(2,128)(2,1)}), bf16[32,2,768]{2,1,0:T(2,128)(2,1)S(1)}, u32[]{:S(2)}, u32[]{:S(2)}) async-start(bf16[32,2,768]{2,1,0:T(2,128)(2,1)} %shard_map.111), calls=%async_computation | async-start | bytes 196608 | tf_op jit(solution)/shard_map/all_to_all | solution.py:90
  19.6 0.0 copy-start
  19.7 2.8 %multiply_add_fusion = (f32[1,1,32,2,768]{4,3,2,1,0:T(2,128)}, f32[1,1,32,2,768]{4,3,2,1,0:T(2,128)}, f32[1,1,32,2,768]{4,3,2,1,0:T(2,128)}) fusion(f32[1,1,32,2,768]{4,3,2,1,0:T(2,128)} %param.8, bf16[1,1,32,2,768]{4,3,2,1,0:T(2,128)(2,1)} %param.11, f32[1,1,32,2,768]{4,3,2,1,0:T(2,128)} %param.9, f32[1,1,32,2,768]{4,3,2,1,0:T(2,128)} %param.10), kind=kLoop, calls=%fused_computation.7 | loop fusion | flops 786432 | bytes 1277952 | tf_op jit(solution)/shard_map/add | solution.py:92
  22.4 5.1 %all-to-all-done = bf16[32,2,768]{2,1,0:T(2,128)(2,1)S(1)} async-done(((bf16[32,2,768]{2,1,0:T(2,128)(2,1)}), bf16[32,2,768]{2,1,0:T(2,128)(2,1)S(1)}, u32[]{:S(2)}, u32[]{:S(2)}) %all-to-all-start) | async-done | bytes 98336 | tf_op jit(solution)/shard_map/all_to_all | solution.py:90
  27.6 16.2 %all_gather.6 = bf16[4,64,768]{2,1,0:T(8,128)(2,1)S(1)} all-gather(bf16[1,64,768]{2,1,0:T(8,128)(2,1)S(1)} %all_gather_reshape.3), channel_id=1, replica_groups=mesh['x_hi'=4,'z'=8,'expert'=32] {'x_hi'}, dimensions={0}, use_global_device_ids=true | all-gather | bytes 491520 | tf_op jit(solution)/shard_map/all_gather | solution.py:94
  43.8 0.1 multiply_convert_fusion
  43.9 40.4 %all-gather.1 = f16[4,512,768]{2,1,0:T(8,128)(2,1)S(1)} all-gather(f16[4,64,768]{2,1,0:T(8,128)(2,1)S(1)} %multiply_convert_fusion), channel_id=1, replica_groups=mesh['x_hi'=4,'z'=8,'expert'=32] {'z'}, dimensions={1}, use_global_device_ids=true | all-gather | bytes 3538944 | tf_op jit(solution)/shard_map/all_gather | solution.py:96
  84.3 0.0 copy-done
  84.3 1.1 %fusion = bf16[4,512,768]{2,1,0:T(8,128)(2,1)S(1)} fusion(bf16[4,512,768]{2,1,0:T(8,128)(2,1)S(1)} %bitcast.14, f16[4,512,768]{2,1,0:T(8,128)(2,1)S(1)} %all-gather.1), kind=kLoop, calls=%fused_computation.1 | loop fusion | flops 7864320 | bytes 9437184 | tf_op jit(solution)/shard_map/convert_element_type | solution.py:99
  85.4 1.7 %shard_map.112 = bf16[2048,768]{1,0:T(8,128)(2,1)} custom-call(bf16[2048,768]{1,0:T(8,128)(2,1)S(1)} %bitcast.12), custom_call_target="tpu_custom_call" | custom-call | tf_op jit(solution)/shard_map/pallas_call | solution.py:101
  (1 shorter events, 0.0 us)
Async XLA Ops:
  2.9 24.7 %all-to-all-start = ((bf16[32,2,768]{2,1,0:T(2,128)(2,1)}), bf16[32,2,768]{2,1,0:T(2,128)(2,1)S(1)}, u32[]{:S(2)}, u32[]{:S(2)}) async-start(bf16[32,2,768]{2,1,0:T(2,128)(2,1)} %shard_map.111), calls=%async_computation | async-start | bytes 196608 | tf_op jit(solution)/shard_map/all_to_all | solution.py:90
  19.6 64.6 %copy-start = (bf16[1,2048,768]{2,1,0:T(8,128)(2,1)S(1)}, bf16[1,2048,768]{2,1,0:T(8,128)(2,1)}, u32[]{:S(2)}) copy-start(bf16[1,2048,768]{2,1,0:T(8,128)(2,1)} %param.15) | copy-start | bytes 9437188
